TPU v7x, 32 devices: a whole 2x2x4 slice. The times are simulated.
32 devices in a mesh: grp: 4 (over z), shard: 8 (over y, x, core).
Axes of the slice: x: 2, y: 2, z: 4, core: 2. Of those that a mesh axis runs over, the one named last changes fastest.
Arguments:
- table: float32 [1024, 8, 128], P('shard')
- table_first: float32 [1024, 8, 128], P('shard'), may hold values from -3 to 3
- table_second: float32 [1024, 8, 128], P('shard')
- slot_table: int32 [1024], P('shard'), may hold values from 0 to 25
- touched: int32 [4, 256], P('grp', 'shard'), may hold values from 0 to 1023, as said below
- emb_grads: bfloat16 [4, 256, 8, 128], P('grp', 'shard'), may hold values from -6 to 6
- block_slot: int32 [1024], replicated, may hold values from 0 to 1023, as said below
- dense_x: bfloat16 [13, 131072], P(None, ('grp', 'shard')), may hold values from -6 to 6
- dense_cot: bfloat16 [131072, 128], P(('grp', 'shard')), may hold values from -0.15625 to 0.15625
- w_one: float32 [13, 512], replicated, may hold values from -1.75 to 1.75
- w_two: float32 [512, 256], replicated, may hold values from -0.25 to 0.25
- w_three: float32 [256, 128], replicated, may hold values from -0.375 to 0.375
- first_one: float32 [13, 512], replicated, may hold values from -3 to 3
- first_two: float32 [512, 256], replicated, may hold values from -3 to 3
- first_three: float32 [256, 128], replicated, may hold values from -3 to 3
- second_one: float32 [13, 512], replicated, may hold values from 0.001 to 0.3
- second_two: float32 [512, 256], replicated, may hold values from 0.001 to 0.3
- second_three: float32 [256, 128], replicated, may hold values from 0.001 to 0.3
Outputs:
- new_table: float32 [1024, 8, 128], P('shard')
- new_table_first: float32 [1024, 8, 128], P('shard')
- new_table_second: float32 [1024, 8, 128], P('shard')
- new_w_one: float32 [13, 512], replicated
- new_w_two: float32 [512, 256], replicated
- new_w_three: float32 [256, 128], replicated
- new_first_one: float32 [13, 512], replicated
- new_first_two: float32 [512, 256], replicated
- new_first_three: float32 [256, 128], replicated
- new_second_one: float32 [13, 512], replicated
- new_second_two: float32 [512, 256], replicated
- new_second_three: float32 [256, 128], replicated
Inputs may be any that keep to these rules, and one draw needn't show every extreme that they name: `touched`: each device's 32 ids are distinct; at most 8 of them have block_slot // 128 equal to any one shard, and in every draw some shard gets exactly 8 from every device. `block_slot`: A permutation of the 1024 slots.
All inputs are finite; a program needn't handle non-finite values.
Results may differ from a plain program's by a relative error of at most 0.0037.
Values may be sent and summed in bfloat16 or wider, within the bound.
A program may use at most 128 MiB of HBM per device.

v0:
```python
import jax
import jax.numpy as jnp
from jax import lax
from jax.sharding import PartitionSpec as P

TABLES = 26
CAP = 8
beta_one = 0.9
beta_two = 0.999
corr_first = 1.0 - 0.9**10
corr_second = 1.0 - 0.999**10
adam_eps = 1e-06
decay_rate = 0.01
learn_rate = 0.1
ratio_eps = 1e-06


def silu_slope(pre_value):
    logistic = jax.nn.sigmoid(pre_value)
    return logistic * (1.0 + pre_value * (1.0 - logistic))


def tower_grads(dense_x, dense_cot, w_one, w_two, w_three):
    w_one_bf = w_one.astype(jnp.bfloat16)
    w_two_bf = w_two.astype(jnp.bfloat16)
    w_three_bf = w_three.astype(jnp.bfloat16)
    pre_one = lax.dot_general(
        dense_x, w_one_bf, (((0,), (0,)), ((), ())), preferred_element_type=jnp.float32
    )
    hidden_one = jax.nn.silu(pre_one).astype(jnp.bfloat16)
    pre_two = jnp.dot(hidden_one, w_two_bf, preferred_element_type=jnp.float32)
    hidden_two = jax.nn.silu(pre_two).astype(jnp.bfloat16)
    grad_three = lax.dot_general(
        hidden_two, dense_cot, (((0,), (0,)), ((), ())), preferred_element_type=jnp.float32
    )
    back_two = (
        lax.dot_general(
            dense_cot, w_three_bf, (((1,), (1,)), ((), ())), preferred_element_type=jnp.float32
        )
        * silu_slope(pre_two)
    ).astype(jnp.bfloat16)
    grad_two = lax.dot_general(
        hidden_one, back_two, (((0,), (0,)), ((), ())), preferred_element_type=jnp.float32
    )
    back_one = (
        lax.dot_general(
            back_two, w_two_bf, (((1,), (1,)), ((), ())), preferred_element_type=jnp.float32
        )
        * silu_slope(pre_one)
    ).astype(jnp.bfloat16)
    grad_one = jnp.dot(dense_x, back_one, preferred_element_type=jnp.float32)
    return (grad_one, grad_two, grad_three)


def lamb_dense(weight, first_in, second_in, gradient):
    first_out = beta_one * first_in + (1.0 - beta_one) * gradient
    second_out = beta_two * second_in + (1.0 - beta_two) * gradient * gradient
    update = (
        first_out / corr_first / (jnp.sqrt(second_out / corr_second) + adam_eps)
        + decay_rate * weight
    )
    trust_ratio = jnp.sqrt(jnp.sum(weight * weight)) / (
        jnp.sqrt(jnp.sum(update * update)) + ratio_eps
    )
    return (weight - learn_rate * trust_ratio * update, first_out, second_out)


def body(
    table,
    table_first,
    table_second,
    slot_table,
    touched,
    emb_grads,
    block_slot,
    dense_x,
    dense_cot,
    w_one,
    w_two,
    w_three,
    first_one,
    first_two,
    first_three,
    second_one,
    second_two,
    second_three,
):
    shards = lax.axis_size("shard")
    local_blocks = table.shape[0]
    block_rows = table.shape[1]
    emb_width = table.shape[2]
    row_width = block_rows * emb_width
    capacity = CAP
    dense_terms = tower_grads(dense_x, dense_cot, w_one, w_two, w_three)
    table_hot = (slot_table[:, None] == jnp.arange(TABLES, dtype=jnp.int32)[None, :]).astype(
        jnp.float32
    )
    row_weight = jnp.sum(table * table, axis=(1, 2))
    part_weight = jnp.dot(row_weight, table_hot, precision=lax.Precision.HIGHEST)
    block_ids = touched[0]
    count_touched = block_ids.shape[0]
    grad_rows = emb_grads[0].reshape(count_touched, row_width)
    slot_index = jnp.take(block_slot, block_ids)
    owner_shard = slot_index // local_blocks
    local_row = slot_index % local_blocks
    owner_hot = (owner_shard[:, None] == jnp.arange(shards, dtype=jnp.int32)[None, :]).astype(
        jnp.int32
    )
    bucket_rank = jnp.cumsum(owner_hot, axis=0) - 1
    bucket_place = jnp.sum(owner_hot * bucket_rank, axis=1)
    send_index = owner_shard * capacity + bucket_place
    picker = jnp.arange(shards * capacity, dtype=jnp.int32)[:, None] == send_index[None, :]
    send_rows = jnp.dot(
        picker.astype(jnp.bfloat16), grad_rows, preferred_element_type=jnp.float32
    ).astype(jnp.bfloat16)
    send_local = jnp.where(
        jnp.any(picker, axis=1), jnp.sum(jnp.where(picker, local_row[None, :], 0), axis=1), -1
    )
    send_rows = send_rows.reshape(shards, capacity, row_width)
    send_local = send_local.reshape(shards, capacity)
    recv_rows, recv_local = (
        lax.all_to_all(send_rows, "shard", split_axis=0, concat_axis=0, tiled=True),
        lax.all_to_all(send_local, "shard", split_axis=0, concat_axis=0, tiled=True),
    )
    piece_rows = lax.all_gather(recv_rows, "grp", axis=0, tiled=True).reshape(-1, row_width)
    piece_locals = lax.all_gather(recv_local, "grp", axis=0, tiled=True).reshape(-1)
    matches = piece_locals[:, None] == jnp.arange(local_blocks, dtype=jnp.int32)[None, :]
    summed = lax.dot_general(
        matches.astype(jnp.bfloat16),
        piece_rows,
        (((0,), (0,)), ((), ())),
        preferred_element_type=jnp.float32,
    )
    counted = jnp.sum(matches.astype(jnp.float32), axis=0)
    emb_grad = summed.reshape(local_blocks, block_rows, emb_width)
    touched_mask = (counted > 0.5)[:, None, None]
    new_first = jnp.where(
        touched_mask, beta_one * table_first + (1.0 - beta_one) * emb_grad, table_first
    )
    new_second = jnp.where(
        touched_mask, beta_two * table_second + (1.0 - beta_two) * emb_grad * emb_grad, table_second
    )
    update = jnp.where(
        touched_mask,
        new_first / corr_first / (jnp.sqrt(new_second / corr_second) + adam_eps)
        + decay_rate * table,
        0.0,
    )
    row_update = jnp.sum(update * update, axis=(1, 2))
    part_update = jnp.dot(row_update, table_hot, precision=lax.Precision.HIGHEST)
    dense_grads = lax.psum((dense_terms[0], dense_terms[1], dense_terms[2]), ("grp", "shard"))
    weight_total, update_total = lax.psum((part_weight, part_update), "shard")
    table_ratio = jnp.sqrt(weight_total) / (jnp.sqrt(update_total) + ratio_eps)
    ratio_rows = jnp.dot(table_hot, table_ratio, precision=lax.Precision.HIGHEST)
    new_table = table - learn_rate * ratio_rows[:, None, None] * update
    layer_one = lamb_dense(w_one, first_one, second_one, dense_grads[0])
    layer_two = lamb_dense(w_two, first_two, second_two, dense_grads[1])
    layer_three = lamb_dense(w_three, first_three, second_three, dense_grads[2])
    return (
        new_table,
        new_first,
        new_second,
        layer_one[0],
        layer_two[0],
        layer_three[0],
        layer_one[1],
        layer_two[1],
        layer_three[1],
        layer_one[2],
        layer_two[2],
        layer_three[2],
    )


def solution(mesh):
    return jax.shard_map(
        body,
        mesh=mesh,
        in_specs=(
            P("shard", None, None),
            P("shard", None, None),
            P("shard", None, None),
            P("shard"),
            P("grp", "shard"),
            P("grp", "shard", None, None),
            P(),
            P(None, ("grp", "shard")),
            P(("grp", "shard"), None),
            P(),
            P(),
            P(),
            P(),
            P(),
            P(),
            P(),
            P(),
            P(),
        ),
        out_specs=(
            P("shard", None, None),
            P("shard", None, None),
            P("shard", None, None),
            P(),
            P(),
            P(),
            P(),
            P(),
            P(),
            P(),
            P(),
            P(),
        ),
        check_vma=False,
    )
```

profile of v0, /device:TPU:0, one launch (start us, length us, event | category | flops | bytes accessed | tf_op | source)
XLA Modules:
  0.0 179.8 jit_solution(11988659728228566340)
XLA Ops:
  7.2 0.7 fusion.31
  7.9 1.4 gather_fusion
  10.0 0.7 fusion.30
  11.2 0.7 select_n.94
  11.9 5.2 %all-to-all-start = ((s32[8,1,8]{2,1,0:T(1,128)}), s32[8,1,8]{2,1,0:T(1,128)S(1)}, u32[]{:S(2)}, u32[]{:S(2)}) async-start(s32[8,1,8]{2,1,0:T(1,128)} %bitcast.9), calls=%async_computation | async-start | bytes 8192 | tf_op jit(solution)/shard_map/all_to_all | solution.py:123
  17.1 6.6 %multiply_convert_fusion.1 = (bf16[4096,512]{1,0:T(8,128)(2,1)S(1)}, f32[4096,512]{1,0:T(8,128)}) fusion(bf16[13,4096]{1,0:T(8,128)(2,1)} %param.25, f32[13,512]{1,0:T(8,128)} %param.27), kind=kOutput, calls=%fused_computation.2 | convolution fusion | flops 65018368 | bytes 12716032 | tf_op jit(solution)/shard_map/dot_general | solution.py:27
  23.7 1.3 fusion.12
  25.0 2.0 %fusion.1 = f32[256,128]{1,0:T(8,128)} fusion(bf16[4096,128]{1,0:T(8,128)(2,1)S(1)} %copy-done, f32[4096,256]{1,0:T(8,128)S(1)} %fusion.12), kind=kOutput, calls=%fused_computation.8 | convolution fusion | flops 273678336 | bytes 5373952 | tf_op jit(solution)/shard_map/dot_general | solution.py:33
  26.9 1.7 fusion
  28.7 1.4 copy-done.19
  30.1 2.1 %fusion.46 = f32[512,256]{1,0:T(8,128)} fusion(bf16[4096,512]{1,0:T(8,128)(2,1)S(1)} %get-tuple-element.94, bf16[4096,256]{1,0:T(8,128)(2,1)S(1)} %fusion), kind=kOutput, calls=%fused_computation.101 | convolution fusion | flops 1073741824 | bytes 6815744 | tf_op jit(solution)/shard_map/dot_general | solution.py:42
  32.4 1.0 multiply_reduce_fusion.3
  33.5 1.0 fusion.3
  34.5 7.7 %fusion.4 = f32[13,512]{1,0:T(8,128)S(1)} fusion(bf16[13,4096]{1,0:T(8,128)(2,1)} %param.25, f32[4096,512]{1,0:T(8,128)} %get-tuple-element.95, bf16[4096,256]{1,0:T(8,128)(2,1)} %copy-done.19, f32[512,256]{1,0:T(8,128)S(1)} %copy-done.1), kind=kOutput, calls=%fused_computation.12 | convolution fusion | flops 1147273216 | bytes 11143168 | tf_op jit(solution)/shard_map/dot_general | solution.py:51
  42.1 41.0 %psum.37 = f32[13,512]{1,0:T(8,128)S(1)} all-reduce(f32[13,512]{1,0:T(8,128)S(1)} %fusion.4), channel_id=1, replica_groups=mesh['grp'=4,'shard'=8] {'grp','shard'}, use_global_device_ids=true, to_apply=%region_10.11 | all-reduce | flops 6656 | bytes 53248 | tf_op jit(solution)/shard_map/psum | solution.py:151
  86.2 1.0 copy.73
  87.4 3.6 %all-to-all-start.1 = ((bf16[8,8,1024]{2,1,0:T(8,128)(2,1)}), bf16[8,8,1024]{2,1,0:T(8,128)(2,1)S(1)}, u32[]{:S(2)}, u32[]{:S(2)}) async-start(bf16[8,8,1024]{2,1,0:T(8,128)(2,1)} %fusion.3), calls=%async_computation.1 | async-start | bytes 262144 | tf_op jit(solution)/shard_map/all_to_all | solution.py:122
  91.0 13.2 %all-gather = s32[32,1,8]{2,1,0:T(1,128)S(1)} all-gather(s32[8,1,8]{2,1,0:T(1,128)S(1)} %all-to-all-done), channel_id=2, replica_groups=mesh['grp'=4,'shard'=8] {'grp'}, dimensions={0}, use_global_device_ids=true | all-gather | bytes 1280 | tf_op jit(solution)/shard_map/all_gather | solution.py:126
  104.7 0.7 reduce.3
  105.7 16.0 %all_gather.7 = bf16[32,8,1024]{2,1,0:T(8,128)(2,1)S(1)} all-gather(bf16[8,8,1024]{2,1,0:T(8,128)(2,1)S(1)} %all-to-all-done.1), channel_id=1, replica_groups=mesh['grp'=4,'shard'=8] {'grp'}, dimensions={0}, use_global_device_ids=true | all-gather | bytes 655360 | tf_op jit(solution)/shard_map/all_gather | solution.py:125
  121.7 1.0 copy.74
  122.7 2.9 %multiply_reduce_fusion.2 = (f32[128]{0:T(128)S(1)}, f32[128,8,128]{0,2,1:T(8,128)}, f32[128,8,128]{0,2,1:T(8,128)}, f32[128,8,128]{0,2,1:T(8,128)S(1)}) fusion(f32[128,8,128]{0,2,1:T(8,128)S(1)} %copy.79, pred[128]{0:T(512)(128)(4,1)S(1)} %broadcast_compare_fusion, f32[128,8,128]{0,2,1:T(8,128)} %copy.73, f32[128,8,128]{0,2,1:T(8,128)S(1)} %copy.76, ...), kind=kOutput, calls=%fused_computation.28 | convolution fusion | flops 69500800 | bytes 3671680 | tf_op jit(solution)/shard_map/dot_general | solution.py:128
  125.8 11.8 %all-reduce.1 = (f32[26]{0:T(128)S(1)}, f32[26]{0:T(128)S(1)}) all-reduce(f32[26]{0:T(128)S(1)} %convolution_bitcast_fusion.1, f32[26]{0:T(128)S(1)} %convolution_bitcast_fusion.2), channel_id=1, replica_groups=mesh['grp'=4,'shard'=8] {'shard'}, use_global_device_ids=true, to_apply=%region_8.9 | all-reduce | flops 52 | bytes 416 | tf_op jit(solution)/shard_map/psum | solution.py:152
  137.8 1.1 multiply_subtract_fusion.1
  138.9 1.0 copy.80
  139.9 2.0 %copy.81 = f32[128,8,128]{2,1,0:T(8,128)} copy(f32[128,8,128]{0,2,1:T(8,128)} %get-tuple-element.90) | data formatting | bytes 1048576
  142.0 1.0 copy.82
  143.0 21.3 %all-reduce.4.cloned.1.call-done = (f32[512,256]{1,0:T(8,128)}, f32[256,128]{1,0:T(8,128)}) async-done(((f32[512,256]{1,0:T(8,128)}, f32[256,128]{1,0:T(8,128)}), (f32[512,256]{1,0:T(8,128)}, f32[256,128]{1,0:T(8,128)})) %all-reduce.4.cloned.1.call-update) | async-done | bytes 655376 | tf_op jit(solution)/shard_map/psum | solution.py:151
  164.2 2.4 %multiply_reduce_fusion = (f32[]{:T(128)}, f32[]{:T(128)}, f32[512,256]{1,0:T(8,128)S(1)}, f32[512,256]{1,0:T(8,128)S(1)}) fusion(f32[512,256]{1,0:T(8,128)S(1)} %copy-done.1, f32[512,256]{1,0:T(8,128)} %get-tuple-element.78, f32[512,256]{1,0:T(8,128)} %param.31, f32[512,256]{1,0:T(8,128)} %param.34), kind=kLoop, calls=%fused_computation.23 | loop fusion | flops 2228222 | bytes 3145736 | tf_op jit(solution)/shard_map/reduce_sum | solution.py:63
  168.1 1.6 multiply_reduce_fusion.4
  171.1 1.1 multiply_subtract_fusion
  172.2 0.7 multiply_subtract_fusion.2
  (63 shorter events, 4.4 us)
Async XLA Ops:
  7.2 17.8 %copy-start = (bf16[4096,128]{1,0:T(8,128)(2,1)S(1)}, bf16[4096,128]{1,0:T(8,128)(2,1)}, u32[]{:S(2)}) copy-start(bf16[4096,128]{1,0:T(8,128)(2,1)} %param.26) | copy-start | bytes 3145732
  11.9 75.5 %all-to-all-start = ((s32[8,1,8]{2,1,0:T(1,128)}), s32[8,1,8]{2,1,0:T(1,128)S(1)}, u32[]{:S(2)}, u32[]{:S(2)}) async-start(s32[8,1,8]{2,1,0:T(1,128)} %bitcast.9), calls=%async_computation | async-start | bytes 8192 | tf_op jit(solution)/shard_map/all_to_all | solution.py:123
  17.1 6.6 %copy-start.1 = (f32[512,256]{1,0:T(8,128)S(1)}, f32[512,256]{1,0:T(8,128)}, u32[]{:S(2)}) copy-start(f32[512,256]{1,0:T(8,128)} %param.28) | copy-start | bytes 1572868
  17.1 147.2 %all-reduce.4.cloned.1.call-start = ((), (), s32[]{:S(2)}) async-start(), calls=%async_computation.2 | async-start | bytes 1310720 | tf_op jit(solution)/shard_map/psum | solution.py:151
  25.0 2.0 %copy-start.7 = (f32[256,128]{1,0:T(8,128)S(1)}, f32[256,128]{1,0:T(8,128)}, u32[]{:S(2)}) copy-start(f32[256,128]{1,0:T(8,128)} %param.29) | copy-start | bytes 393220
  28.7 1.4 copy-start.19
  30.1 2.1 %copy-start.2 = (f32[128,8,128]{2,1,0:T(8,128)S(1)}, f32[128,8,128]{2,1,0:T(8,128)}, u32[]{:S(2)}) copy-start(f32[128,8,128]{2,1,0:T(8,128)} %param.18) | copy-start | bytes 1572868
  30.1 3.4 %copy-start.15 = (bf16[1,32,8,128]{3,2,1,0:T(8,128)(2,1)S(1)}, bf16[1,32,8,128]{3,2,1,0:T(8,128)(2,1)}, u32[]{:S(2)}) copy-start(bf16[1,32,8,128]{3,2,1,0:T(8,128)(2,1)} %param.23) | copy-start | bytes 196612
  34.4 48.7 %copy-start.12 = (f32[13,512]{1,0:T(8,128)S(1)}, f32[13,512]{1,0:T(8,128)}, u32[]{:S(2)}) copy-start(f32[13,512]{1,0:T(8,128)} %param.27) | copy-start | bytes 79876
  34.4 48.7 %copy-start.16 = (f32[13,512]{1,0:T(8,128)S(1)}, f32[13,512]{1,0:T(8,128)}, u32[]{:S(2)}) copy-start(f32[13,512]{1,0:T(8,128)} %param.30) | copy-start | bytes 79876
  34.4 48.8 %copy-start.17 = (f32[13,512]{1,0:T(8,128)S(1)}, f32[13,512]{1,0:T(8,128)}, u32[]{:S(2)}) copy-start(f32[13,512]{1,0:T(8,128)} %param.33) | copy-start | bytes 79876
  34.4 50.8 %copy-start.18 = (s32[128]{0:T(128)S(1)}, s32[128]{0:T(128)}, u32[]{:S(2)}) copy-start(s32[128]{0:T(128)} %param.21) | copy-start | bytes 1540
  34.4 51.7 %copy-start.5 = (f32[128,8,128]{2,1,0:T(8,128)S(1)}, f32[128,8,128]{2,1,0:T(8,128)}, u32[]{:S(2)}) copy-start(f32[128,8,128]{2,1,0:T(8,128)} %param.19) | copy-start | bytes 1572868
  34.4 52.7 %copy-start.6 = (f32[128,8,128]{2,1,0:T(8,128)S(1)}, f32[128,8,128]{2,1,0:T(8,128)}, u32[]{:S(2)}) copy-start(f32[128,8,128]{2,1,0:T(8,128)} %param.20) | copy-start | bytes 1572868
  83.8 21.8 %copy-start.13 = (f32[13,512]{1,0:T(8,128)}, f32[13,512]{1,0:T(8,128)S(1)}, u32[]{:S(2)}) copy-start(f32[13,512]{1,0:T(8,128)S(1)} %get-tuple-element.86) | copy-start | bytes 79876
  83.8 21.8 %copy-start.14 = (f32[13,512]{1,0:T(8,128)}, f32[13,512]{1,0:T(8,128)S(1)}, u32[]{:S(2)}) copy-start(f32[13,512]{1,0:T(8,128)S(1)} %get-tuple-element.87) | copy-start | bytes 79876
  87.4 18.2 %all-to-all-start.1 = ((bf16[8,8,1024]{2,1,0:T(8,128)(2,1)}), bf16[8,8,1024]{2,1,0:T(8,128)(2,1)S(1)}, u32[]{:S(2)}, u32[]{:S(2)}) async-start(bf16[8,8,1024]{2,1,0:T(8,128)(2,1)} %fusion.3), calls=%async_computation.1 | async-start | bytes 262144 | tf_op jit(solution)/shard_map/all_to_all | solution.py:122
  125.6 42.5 %copy-start.10 = (f32[256,128]{1,0:T(8,128)S(1)}, f32[256,128]{1,0:T(8,128)}, u32[]{:S(2)}) copy-start(f32[256,128]{1,0:T(8,128)} %param.32) | copy-start | bytes 393220
  125.6 42.5 %copy-start.11 = (f32[256,128]{1,0:T(8,128)S(1)}, f32[256,128]{1,0:T(8,128)}, u32[]{:S(2)}) copy-start(f32[256,128]{1,0:T(8,128)} %param.35) | copy-start | bytes 393220
  166.6 6.3 %copy-start.3 = (f32[512,256]{1,0:T(8,128)}, f32[512,256]{1,0:T(8,128)S(1)}, u32[]{:S(2)}) copy-start(f32[512,256]{1,0:T(8,128)S(1)} %get-tuple-element.84) | copy-start | bytes 1572868
  166.6 6.3 %copy-start.4 = (f32[512,256]{1,0:T(8,128)}, f32[512,256]{1,0:T(8,128)S(1)}, u32[]{:S(2)}) copy-start(f32[512,256]{1,0:T(8,128)S(1)} %get-tuple-element.85) | copy-start | bytes 1572868
  169.7 3.2 %copy-start.8 = (f32[256,128]{1,0:T(8,128)}, f32[256,128]{1,0:T(8,128)S(1)}, u32[]{:S(2)}) copy-start(f32[256,128]{1,0:T(8,128)S(1)} %get-tuple-element.82) | copy-start | bytes 393220
  169.7 3.2 %copy-start.9 = (f32[256,128]{1,0:T(8,128)}, f32[256,128]{1,0:T(8,128)S(1)}, u32[]{:S(2)}) copy-start(f32[256,128]{1,0:T(8,128)S(1)} %get-tuple-element.83) | copy-start | bytes 393220
Sparse Core Ops, SparseCore 0:
  32.3 131.8 all-reduce.3
where the time goes:
time: 180 us
  blocking collectives  82 us (46%)
  matrix products  25.8 us (14%)
  waiting for transfers between devices  21.3 us (12%)
  between operations  18.6 us (10%)
  other arithmetic  12.7 us (7%)
  local copies, waits for them, and re-layouts  10.6 us (6%)
  starting transfers between devices  8.81 us (5%)
    psum x1, blocking collectives, body(): lax.psum((dense_terms[0], dense_terms[1], dense_terms[2]), ('grp', 'shard'))  41 us
    psum x1, waiting for transfers between devices, body(): lax.psum((dense_terms[0], dense_terms[1], dense_terms[2]), ('grp', 'shard'))  21.3 us
    all_gather x1, blocking collectives, body(): lax.all_gather(recv_rows, 'grp', axis=0, tiled=True).reshape(-1, row_width)  16 us
    all_gather x1, blocking collectives, body(): lax.all_gather(recv_local, 'grp', axis=0, tiled=True).reshape(-1)  13.2 us
    psum x1, blocking collectives, body(): weight_total, update_total = lax.psum((part_weight, part_update), 'shard')  11.8 us
    dot_general x1, matrix products, tower_grads(): grad_one = jnp.dot(dense_x, back_one, preferred_element_type=jnp.float32)  7.68 us
    unnamed x46, local copies, waits for them, and re-layouts  6.98 us
    dot_general x1, matrix products, tower_grads(): lax.dot_general(dense_x, w_one_bf, (((0,), (0,)), ((), ())), preferred_el...  6.56 us
  transfers between devices with their start and end apart: 3, of which 1 were waited for; matrix products, arithmetic and copies ran while one was open for 21% of the time, Pallas kernels for 0%

commit v1 on v0

--- a/solution.py
+++ b/solution.py
@@ -148,7 +148,9 @@
     )
     row_update = jnp.sum(update * update, axis=(1, 2))
     part_update = jnp.dot(row_update, table_hot, precision=lax.Precision.HIGHEST)
-    dense_grads = lax.psum((dense_terms[0], dense_terms[1], dense_terms[2]), ("grp", "shard"))
+    dense_grads = lax.psum(
+        lax.psum((dense_terms[0], dense_terms[1], dense_terms[2]), "shard"), "grp"
+    )
     weight_total, update_total = lax.psum((part_weight, part_update), "shard")
     table_ratio = jnp.sqrt(weight_total) / (jnp.sqrt(update_total) + ratio_eps)
     ratio_rows = jnp.dot(table_hot, table_ratio, precision=lax.Precision.HIGHEST)

time: 180 us -> 183 us (1.017)
  blocking collectives: 82 us -> 71 us
  waiting for transfers between devices: 21.3 us -> 31.2 us
  other arithmetic: 12.7 us -> 14.9 us
    psum x1, blocking collectives: 41 us -> 18.2 us  [body(): lax.psum(lax.psum((dense_terms[0], dense_terms[1], dense_terms[2]), 'shar...]
    psum x1, blocking collectives: 11.8 us -> 23.9 us  [body(): weight_total, update_total = lax.psum((part_weight, part_update), 'shard')]
    psum x1 -> x2, waiting for transfers between devices: 21.3 us -> 31.2 us  [the longest x1 31.2 us: body(): lax.psum(lax.psum((dense_terms[0], dense_terms[1], dense_terms[2]), 'shar...]
    unnamed x46 -> x38, local copies, waits for them, and re-layouts: 6.98 us -> 7.01 us
  transfers between devices with their start and end apart: 3 -> 4, of which waited for: 1 -> 1; matrix products, arithmetic and copies ran while one was open for 21% -> 22% of each run, Pallas kernels for 0% -> 0%
where the time goes in v1:
time: 183 us; the launch traced here: 182 us
  blocking collectives  71 us (39%)
  waiting for transfers between devices  31.2 us (17%)
  matrix products  26.4 us (14%)
  between operations  18.5 us (10%)
  other arithmetic  14.9 us (8%)
  local copies, waits for them, and re-layouts  10.7 us (6%)
  starting transfers between devices  9.45 us (5%)
    psum x1, waiting for transfers between devices, body(): lax.psum(lax.psum((dense_terms[0], dense_terms[1], dense_terms[2]), 'shar...  31.2 us
    psum x1, blocking collectives, body(): weight_total, update_total = lax.psum((part_weight, part_update), 'shard')  23.9 us
    psum x1, blocking collectives, body(): lax.psum(lax.psum((dense_terms[0], dense_terms[1], dense_terms[2]), 'shar...  18.2 us
    all_gather x1, blocking collectives, body(): lax.all_gather(recv_rows, 'grp', axis=0, tiled=True).reshape(-1, row_width)  15.5 us
    all_gather x1, blocking collectives, body(): lax.all_gather(recv_local, 'grp', axis=0, tiled=True).reshape(-1)  13.4 us
    dot_general x1, matrix products, tower_grads(): grad_one = jnp.dot(dense_x, back_one, preferred_element_type=jnp.float32)  8.35 us
    unnamed x38, local copies, waits for them, and re-layouts  7.01 us
    dot_general x1, matrix products, tower_grads(): lax.dot_general(dense_x, w_one_bf, (((0,), (0,)), ((), ())), preferred_el...  6.56 us
  transfers between devices with their start and end apart: 4, of which 1 were waited for; matrix products, arithmetic and copies ran while one was open for 22% of the time, Pallas kernels for 0%

profile of v1, /device:TPU:0, one launch (start us, length us, event | category | flops | bytes accessed | tf_op | source)
XLA Modules:
  0.0 182.1 jit_solution(14921380239094980243)
XLA Ops:
  7.2 0.7 fusion.31
  7.9 1.4 gather_fusion
  11.9 5.2 %all-to-all-start = ((s32[8,1,8]{2,1,0:T(1,128)}), s32[8,1,8]{2,1,0:T(1,128)S(1)}, u32[]{:S(2)}, u32[]{:S(2)}) async-start(s32[8,1,8]{2,1,0:T(1,128)} %bitcast.9), calls=%async_computation | async-start | bytes 8192 | tf_op jit(solution)/shard_map/all_to_all | solution.py:123
  17.1 6.6 %multiply_convert_fusion.1 = (bf16[4096,512]{1,0:T(8,128)(2,1)S(1)}, f32[4096,512]{1,0:T(8,128)}) fusion(bf16[13,4096]{1,0:T(8,128)(2,1)} %param.25, f32[13,512]{1,0:T(8,128)} %param.27), kind=kOutput, calls=%fused_computation.2 | convolution fusion | flops 65018368 | bytes 12716032 | tf_op jit(solution)/shard_map/dot_general | solution.py:27
  23.7 1.3 fusion.12
  25.0 2.0 %fusion.1 = f32[256,128]{1,0:T(8,128)} fusion(bf16[4096,128]{1,0:T(8,128)(2,1)S(1)} %copy-done, f32[4096,256]{1,0:T(8,128)S(1)} %fusion.12), kind=kOutput, calls=%fused_computation.8 | convolution fusion | flops 273678336 | bytes 5373952 | tf_op jit(solution)/shard_map/dot_general | solution.py:33
  26.9 1.7 fusion
  28.7 1.4 copy-done.15
  30.1 2.1 %fusion.46 = f32[512,256]{1,0:T(8,128)} fusion(bf16[4096,512]{1,0:T(8,128)(2,1)S(1)} %get-tuple-element.97, bf16[4096,256]{1,0:T(8,128)(2,1)S(1)} %fusion), kind=kOutput, calls=%fused_computation.101 | convolution fusion | flops 1073741824 | bytes 6815744 | tf_op jit(solution)/shard_map/dot_general | solution.py:42
  32.4 1.0 multiply_reduce_fusion.3
  33.5 1.0 fusion.3
  34.4 8.4 %fusion.4 = f32[13,512]{1,0:T(8,128)} fusion(bf16[13,4096]{1,0:T(8,128)(2,1)S(1)} %copy-done.13, f32[4096,512]{1,0:T(8,128)} %get-tuple-element.98, bf16[4096,256]{1,0:T(8,128)(2,1)} %copy-done.15, f32[512,256]{1,0:T(8,128)S(1)} %copy-done.1), kind=kOutput, calls=%fused_computation.12 | convolution fusion | flops 1147273216 | bytes 11143168 | tf_op jit(solution)/shard_map/dot_general | solution.py:51
  43.0 1.1 copy.73
  44.3 4.2 %all-to-all-start.1 = ((bf16[8,8,1024]{2,1,0:T(8,128)(2,1)}), bf16[8,8,1024]{2,1,0:T(8,128)(2,1)S(1)}, u32[]{:S(2)}, u32[]{:S(2)}) async-start(bf16[8,8,1024]{2,1,0:T(8,128)(2,1)} %fusion.3), calls=%async_computation.1 | async-start | bytes 262144 | tf_op jit(solution)/shard_map/all_to_all | solution.py:122
  48.5 13.4 %all-gather = s32[32,1,8]{2,1,0:T(1,128)S(1)} all-gather(s32[8,1,8]{2,1,0:T(1,128)S(1)} %all-to-all-done), channel_id=2, replica_groups=mesh['grp'=4,'shard'=8] {'grp'}, dimensions={0}, use_global_device_ids=true | all-gather | bytes 1280 | tf_op jit(solution)/shard_map/all_gather | solution.py:126
  62.4 0.7 reduce.3
  63.4 15.5 %all_gather.7 = bf16[32,8,1024]{2,1,0:T(8,128)(2,1)S(1)} all-gather(bf16[8,8,1024]{2,1,0:T(8,128)(2,1)S(1)} %all-to-all-done.1), channel_id=1, replica_groups=mesh['grp'=4,'shard'=8] {'grp'}, dimensions={0}, use_global_device_ids=true | all-gather | bytes 655360 | tf_op jit(solution)/shard_map/all_gather | solution.py:125
  78.8 1.0 copy.74
  79.8 2.9 %multiply_reduce_fusion.2 = (f32[128]{0:T(128)S(1)}, f32[128,8,128]{0,2,1:T(8,128)}, f32[128,8,128]{0,2,1:T(8,128)}, f32[128,8,128]{0,2,1:T(8,128)S(1)}) fusion(f32[128,8,128]{0,2,1:T(8,128)S(1)} %copy.79, pred[128]{0:T(512)(128)(4,1)S(1)} %broadcast_compare_fusion, f32[128,8,128]{0,2,1:T(8,128)} %copy.73, f32[128,8,128]{0,2,1:T(8,128)S(1)} %copy.76, ...), kind=kOutput, calls=%fused_computation.28 | convolution fusion | flops 69500800 | bytes 3671680 | tf_op jit(solution)/shard_map/dot_general | solution.py:128
  82.9 23.9 %all-reduce = (f32[26]{0:T(128)S(1)}, f32[26]{0:T(128)S(1)}, f32[13,512]{1,0:T(8,128)S(1)}) all-reduce(f32[26]{0:T(128)S(1)} %convolution_bitcast_fusion.1, f32[26]{0:T(128)S(1)} %convolution_bitcast_fusion.2, f32[13,512]{1,0:T(8,128)} %fusion.4), channel_id=1, replica_groups=mesh['grp'=4,'shard'=8] {'shard'}, use_global_device_ids=true, to_apply=%region_8.9 | all-reduce | flops 6708 | bytes 53664 | tf_op jit(solution)/shard_map/psum | solution.py:154
  106.8 18.2 %psum.59 = f32[13,512]{1,0:T(8,128)S(1)} all-reduce(f32[13,512]{1,0:T(8,128)S(1)} %get-tuple-element.80), channel_id=1, replica_groups=mesh['grp'=4,'shard'=8] {'grp'}, use_global_device_ids=true, to_apply=%region_11.12 | all-reduce | flops 6656 | bytes 53248 | tf_op jit(solution)/shard_map/psum | solution.py:151
  125.0 2.0 %multiply_reduce_fusion.6 = (f32[]{:T(128)}, f32[]{:T(128)}, f32[13,512]{1,0:T(8,128)}, f32[13,512]{1,0:T(8,128)}) fusion(f32[13,512]{1,0:T(8,128)} %param.27, f32[13,512]{1,0:T(8,128)S(1)} %psum.59, f32[13,512]{1,0:T(8,128)} %param.30, f32[13,512]{1,0:T(8,128)} %param.33), kind=kLoop, calls=%fused_computation.54 | loop fusion | flops 113150 | bytes 159752 | tf_op jit(solution)/shard_map/reduce_sum | solution.py:63
  128.7 1.2 multiply_subtract_fusion.1
  129.9 1.0 copy.80
  130.8 2.1 %copy.81 = f32[128,8,128]{2,1,0:T(8,128)} copy(f32[128,8,128]{0,2,1:T(8,128)} %get-tuple-element.93) | data formatting | bytes 1048576
  132.9 1.0 copy.82
  134.0 1.4 multiply_subtract_fusion.3
  135.4 31.2 %all-reduce.8.cloned.1.call-done = (f32[512,256]{1,0:T(8,128)}, f32[256,128]{1,0:T(8,128)}) async-done(((f32[512,256]{1,0:T(8,128)}, f32[256,128]{1,0:T(8,128)}), (f32[512,256]{1,0:T(8,128)}, f32[256,128]{1,0:T(8,128)})) %all-reduce.8.cloned.1.call-update) | async-done | bytes 655376 | tf_op jit(solution)/shard_map/psum | solution.py:151
  166.6 1.6 multiply_reduce_fusion.4
  169.6 2.4 %multiply_reduce_fusion = (f32[]{:T(128)}, f32[]{:T(128)}, f32[512,256]{1,0:T(8,128)S(1)}, f32[512,256]{1,0:T(8,128)S(1)}) fusion(f32[512,256]{1,0:T(8,128)S(1)} %copy-done.1, f32[512,256]{1,0:T(8,128)} %get-tuple-element.83, f32[512,256]{1,0:T(8,128)} %param.31, f32[512,256]{1,0:T(8,128)} %param.34), kind=kLoop, calls=%fused_computation.23 | loop fusion | flops 2228222 | bytes 3145736 | tf_op jit(solution)/shard_map/reduce_sum | solution.py:63
  173.5 0.7 multiply_subtract_fusion.2
  174.2 1.1 multiply_subtract_fusion
  (58 shorter events, 4.5 us)
Async XLA Ops:
  7.2 17.8 %copy-start = (bf16[4096,128]{1,0:T(8,128)(2,1)S(1)}, bf16[4096,128]{1,0:T(8,128)(2,1)}, u32[]{:S(2)}) copy-start(bf16[4096,128]{1,0:T(8,128)(2,1)} %param.26) | copy-start | bytes 3145732
  11.9 32.4 %all-to-all-start = ((s32[8,1,8]{2,1,0:T(1,128)}), s32[8,1,8]{2,1,0:T(1,128)S(1)}, u32[]{:S(2)}, u32[]{:S(2)}) async-start(s32[8,1,8]{2,1,0:T(1,128)} %bitcast.9), calls=%async_computation | async-start | bytes 8192 | tf_op jit(solution)/shard_map/all_to_all | solution.py:123
  17.1 6.6 %copy-start.1 = (f32[512,256]{1,0:T(8,128)S(1)}, f32[512,256]{1,0:T(8,128)}, u32[]{:S(2)}) copy-start(f32[512,256]{1,0:T(8,128)} %param.28) | copy-start | bytes 1572868
  17.1 111.4 %all-reduce.6.cloned.1.call-start = ((), (), s32[]{:S(2)}) async-start(), calls=%async_computation.2 | async-start | bytes 1310720 | tf_op jit(solution)/shard_map/psum | solution.py:152
  25.0 2.0 %copy-start.7 = (f32[256,128]{1,0:T(8,128)S(1)}, f32[256,128]{1,0:T(8,128)}, u32[]{:S(2)}) copy-start(f32[256,128]{1,0:T(8,128)} %param.29) | copy-start | bytes 393220
  28.7 1.4 copy-start.15
  30.1 2.1 %copy-start.2 = (f32[128,8,128]{2,1,0:T(8,128)S(1)}, f32[128,8,128]{2,1,0:T(8,128)}, u32[]{:S(2)}) copy-start(f32[128,8,128]{2,1,0:T(8,128)} %param.18) | copy-start | bytes 1572868
  30.1 3.4 %copy-start.12 = (bf16[1,32,8,128]{3,2,1,0:T(8,128)(2,1)S(1)}, bf16[1,32,8,128]{3,2,1,0:T(8,128)(2,1)}, u32[]{:S(2)}) copy-start(bf16[1,32,8,128]{3,2,1,0:T(8,128)(2,1)} %param.23) | copy-start | bytes 196612
  30.1 4.3 %copy-start.13 = (bf16[13,4096]{1,0:T(8,128)(2,1)S(1)}, bf16[13,4096]{1,0:T(8,128)(2,1)}, u32[]{:S(2)}) copy-start(bf16[13,4096]{1,0:T(8,128)(2,1)} %param.25) | copy-start | bytes 319492
  34.4 8.4 %copy-start.14 = (s32[128]{0:T(128)S(1)}, s32[128]{0:T(128)}, u32[]{:S(2)}) copy-start(s32[128]{0:T(128)} %param.21) | copy-start | bytes 1540
  34.4 8.6 %copy-start.5 = (f32[128,8,128]{2,1,0:T(8,128)S(1)}, f32[128,8,128]{2,1,0:T(8,128)}, u32[]{:S(2)}) copy-start(f32[128,8,128]{2,1,0:T(8,128)} %param.19) | copy-start | bytes 1572868
  34.4 9.6 %copy-start.6 = (f32[128,8,128]{2,1,0:T(8,128)S(1)}, f32[128,8,128]{2,1,0:T(8,128)}, u32[]{:S(2)}) copy-start(f32[128,8,128]{2,1,0:T(8,128)} %param.20) | copy-start | bytes 1572868
  44.3 19.1 %all-to-all-start.1 = ((bf16[8,8,1024]{2,1,0:T(8,128)(2,1)}), bf16[8,8,1024]{2,1,0:T(8,128)(2,1)S(1)}, u32[]{:S(2)}, u32[]{:S(2)}) async-start(bf16[8,8,1024]{2,1,0:T(8,128)(2,1)} %fusion.3), calls=%async_computation.1 | async-start | bytes 262144 | tf_op jit(solution)/shard_map/all_to_all | solution.py:122
  48.4 118.1 %all-reduce.8.cloned.1.call-start = ((), (), s32[]{:S(2)}) async-start(), calls=%async_computation.3 | async-start | bytes 1310720 | tf_op jit(solution)/shard_map/psum | solution.py:151
  79.8 86.7 %copy-start.10 = (f32[256,128]{1,0:T(8,128)S(1)}, f32[256,128]{1,0:T(8,128)}, u32[]{:S(2)}) copy-start(f32[256,128]{1,0:T(8,128)} %param.32) | copy-start | bytes 393220
  82.7 83.8 %copy-start.11 = (f32[256,128]{1,0:T(8,128)S(1)}, f32[256,128]{1,0:T(8,128)}, u32[]{:S(2)}) copy-start(f32[256,128]{1,0:T(8,128)} %param.35) | copy-start | bytes 393220
  168.2 7.1 %copy-start.8 = (f32[256,128]{1,0:T(8,128)}, f32[256,128]{1,0:T(8,128)S(1)}, u32[]{:S(2)}) copy-start(f32[256,128]{1,0:T(8,128)S(1)} %get-tuple-element.85) | copy-start | bytes 393220
  168.2 7.1 %copy-start.9 = (f32[256,128]{1,0:T(8,128)}, f32[256,128]{1,0:T(8,128)S(1)}, u32[]{:S(2)}) copy-start(f32[256,128]{1,0:T(8,128)S(1)} %get-tuple-element.86) | copy-start | bytes 393220
  172.0 3.2 %copy-start.3 = (f32[512,256]{1,0:T(8,128)}, f32[512,256]{1,0:T(8,128)S(1)}, u32[]{:S(2)}) copy-start(f32[512,256]{1,0:T(8,128)S(1)} %get-tuple-element.87) | copy-start | bytes 1572868
  172.0 3.2 %copy-start.4 = (f32[512,256]{1,0:T(8,128)}, f32[512,256]{1,0:T(8,128)S(1)}, u32[]{:S(2)}) copy-start(f32[512,256]{1,0:T(8,128)S(1)} %get-tuple-element.88) | copy-start | bytes 1572868
Sparse Core Ops, SparseCore 0:
  32.3 56.9 all-reduce.5
  128.6 37.9 all-reduce.7
